TPU v7x, 32 devices: a whole 2x2x4 slice. The times are simulated.
32 devices in a mesh: blk: 8 (over y, x, core), feat: 4 (over z).
Axes of the slice: x: 2, y: 2, z: 4, core: 2. Of those that a mesh axis runs over, the one named last changes fastest.
Arguments:
- node_feats: bfloat16 [8192, 512], P('blk', 'feat'), may hold values from -6 to 6
- weight: bfloat16 [512, 512], P(None, 'feat'), may hold values from -0.25 to 0.25
- tile_value: bfloat16 [8, 5, 8, 128, 128], P('blk'), may hold values from -0.75 to 0.75
- tile_row: int32 [8, 5, 8], P('blk'), may hold values from 0 to 7
- tile_col: int32 [8, 5, 8], P('blk'), may hold values from 0 to 7
- tile_count: int32 [8, 5], P('blk'), may hold values from 2 to 8, as said below
- grad_out: bfloat16 [8192, 512], P('blk', 'feat'), may hold values from -6 to 6
Outputs:
- output_y: bfloat16 [8192, 512], P('blk', 'feat')
- grad_x: bfloat16 [8192, 512], P('blk', 'feat')
- grad_w: float32 [512, 512], P(None, 'feat')
Inputs may be any that keep to these rules, and one draw needn't show every extreme that they name: `tile_count`: in every draw one owner has all 8 slots live for every distance; owners differ in how many tiles they hold.
All inputs are finite; a program needn't handle non-finite values.
Results may differ from a plain program's by a relative error of at most 0.0062.
Values may be sent and summed in bfloat16 or wider, within the bound.
A program may use at most 64 MiB of HBM per device.

v0:
```python
import jax
import jax.numpy as jnp
from jax import lax
from jax.sharding import PartitionSpec as P


def shifted(block, axis, distance):
    devices = range(lax.axis_size(axis))
    route = [((i - distance) % len(devices), i) for i in devices]
    return lax.ppermute(block, axis, route)


def on_device(node_feats, weight, tile_value, tile_row, tile_col, tile_count, grad_out):
    tile_side = tile_value.shape[-1]
    blocks = node_feats.shape[0] // tile_side
    feat_width = weight.shape[1]
    offsets = tile_value.shape[1]
    reach_count = (offsets - 1) // 2
    slot_ids = jnp.arange(tile_value.shape[2], dtype=jnp.int32)
    block_ids = jnp.arange(blocks, dtype=jnp.int32)
    live_slots = slot_ids[None, :] < tile_count[0][:, None]
    row_onehot = (
        (tile_row[0][:, None, :] == block_ids[None, :, None]) & live_slots[:, None, :]
    ).astype(jnp.float32)
    col_onehot = (
        (tile_col[0][:, None, :] == block_ids[None, :, None]) & live_slots[:, None, :]
    ).astype(jnp.float32)
    full_feats = lax.all_gather(node_feats, "feat", axis=1, tiled=True)
    hidden = jnp.dot(full_feats, weight, preferred_element_type=jnp.float32).astype(jnp.bfloat16)
    panel_own = hidden.reshape(blocks, tile_side, feat_width)
    wanted_lists = {}
    picked = jnp.take(panel_own, tile_col[0, reach_count], axis=0)
    gather_product = jnp.einsum(
        "sij,sjf->sif", tile_value[0, reach_count], picked, preferred_element_type=jnp.float32
    )
    aggregate = jnp.einsum(
        "rs,sif->rif", row_onehot[reach_count], gather_product, precision=lax.Precision.HIGHEST
    )
    for distance in range(-reach_count, reach_count + 1):
        if distance != 0:
            offset = distance + reach_count
            wanted = shifted(tile_col[0, offset], "blk", distance)
            wanted_lists[distance] = wanted
            sent_blocks = jnp.take(panel_own, wanted, axis=0)
            arrived = shifted(sent_blocks, "blk", -distance)
            product = jnp.einsum(
                "sij,sjf->sif", tile_value[0, offset], arrived, preferred_element_type=jnp.float32
            )
            aggregate = aggregate + jnp.einsum(
                "rs,sif->rif", row_onehot[offset], product, precision=lax.Precision.HIGHEST
            )
    preact = aggregate.reshape(blocks * tile_side, feat_width) + hidden.astype(jnp.float32)
    output_y = jax.nn.silu(preact).astype(jnp.bfloat16)
    sigmoid_pre = jax.nn.sigmoid(preact)
    slope_term = sigmoid_pre * (1.0 + preact * (1.0 - sigmoid_pre))
    grad_pre = (grad_out.astype(jnp.float32) * slope_term).astype(jnp.bfloat16)
    grad_blocks = grad_pre.reshape(blocks, tile_side, feat_width)

    def slot_products(offset):
        picked = jnp.take(grad_blocks, tile_row[0, offset], axis=0)
        return jnp.einsum(
            "sji,sjf->sif", tile_value[0, offset], picked, preferred_element_type=jnp.float32
        )

    transposed = jnp.einsum(
        "cs,sif->cif",
        col_onehot[reach_count],
        slot_products(reach_count),
        precision=lax.Precision.HIGHEST,
    )
    for distance in range(-reach_count, reach_count + 1):
        if distance != 0:
            offset = distance + reach_count
            masked = slot_products(offset) * live_slots[offset][:, None, None].astype(jnp.float32)
            received = shifted(masked, "blk", distance)
            target_onehot = (wanted_lists[distance][None, :] == block_ids[:, None]).astype(
                jnp.float32
            )
            transposed = transposed + jnp.einsum(
                "cs,sif->cif", target_onehot, received, precision=lax.Precision.HIGHEST
            )
    grad_hidden = (
        grad_pre.astype(jnp.float32) + transposed.reshape(blocks * tile_side, feat_width)
    ).astype(jnp.bfloat16)
    weight_term = lax.dot_general(
        full_feats, grad_hidden, (((0,), (0,)), ((), ())), preferred_element_type=jnp.float32
    )
    grad_w = lax.psum(weight_term, "blk")
    partial_grad = lax.dot_general(
        grad_hidden, weight, (((1,), (1,)), ((), ())), preferred_element_type=jnp.float32
    )
    grad_x = lax.psum_scatter(partial_grad, "feat", scatter_dimension=1, tiled=True).astype(
        jnp.bfloat16
    )
    return (output_y, grad_x, grad_w)


def solution(mesh):
    return jax.shard_map(
        on_device,
        mesh=mesh,
        in_specs=(
            P("blk", "feat"),
            P(None, "feat"),
            P("blk", None, None, None, None),
            P("blk", None, None),
            P("blk", None, None),
            P("blk", None),
            P("blk", "feat"),
        ),
        out_specs=(P("blk", "feat"), P("blk", "feat"), P(None, "feat")),
        check_vma=False,
    )
```

profile of v0, /device:TPU:0, one launch (start us, length us, event | category | flops | bytes accessed | tf_op | source)
XLA Modules:
  0.0 216.4 jit_solution(13034620834880448403)
XLA Ops:
  8.7 3.9 %collective-permute-start = (s32[8]{0:T(128)S(1)}, s32[8]{0:T(128)S(1)}, u32[]{:S(2)}, u32[]{:S(2)}) collective-permute-start(s32[8]{0:T(128)S(1)} %get-tuple-element.32), channel_id=1, source_target_pairs={{8,0},{12,4},{16,8},{20,12},{24,16},{28,20},{0,24},{4,28},{9,1},{1... | collective-permute-start | bytes 104 | tf_op jit(solution)/shard_map/ppermute | solution.py:10
  15.1 1.3 compare_and_fusion.2
  22.6 19.6 %all-gather.2.cloned.1.call-done = bf16[1024,512]{1,0:T(8,128)(2,1)} async-done(((bf16[1024,128]{1,0:T(8,128)(2,1)}), bf16[1024,512]{1,0:T(8,128)(2,1)}) %all-gather.2.cloned.1.call-update) | async-done | bytes 1048592 | tf_op jit(solution)/shard_map/all_gather | solution.py:28
  42.2 1.7 convolution_convert_fusion
  49.6 2.6 %collective-permute-start.5 = (bf16[8,128,128]{2,1,0:T(8,128)(2,1)}, bf16[8,128,128]{2,1,0:T(8,128)(2,1)}, u32[]{:S(2)}, u32[]{:S(2)}) collective-permute-start(bf16[8,128,128]{2,1,0:T(8,128)(2,1)} %broadcast_select_fusion.1), channel_id=1, source_target_pairs={{4,0},{8,4},{12,8},{16,12},{20,16},{24,20},{28,24},{0,28},{5,1},{9... | collective-permute-start | bytes 786440 | tf_op jit(solution)/shard_map/ppermute | solution.py:10
  53.7 1.3 collective-permute-start.7
  55.4 1.3 fusion.25
  56.7 1.3 fusion.21
  58.0 1.0 copy.14
  59.0 1.0 copy.15
  60.0 1.3 fusion.17
  61.3 1.0 copy.16
  62.3 1.8 collective-permute-done.7
  64.4 1.0 copy.17
  68.5 1.0 multiply_convert_fusion
  71.0 0.9 multiply_bitcast_fusion.3
  71.9 1.5 collective-permute-start.8
  75.3 0.9 multiply_bitcast_fusion.1
  81.3 2.4 %collective-permute-start.9 = (f32[8,128,128]{2,0,1:T(8,128)S(1)}, f32[8,128,128]{2,0,1:T(8,128)S(1)}, u32[]{:S(2)}, u32[]{:S(2)}) collective-permute-start(f32[8,128,128]{2,0,1:T(8,128)S(1)} %multiply_bitcast_fusion.2), channel_id=1, source_target_pairs={{4,0},{8,4},{12,8},{16,12},{20,16},{24,20},{28,24},{0,28},{5,1},{9... | collective-permute-start | bytes 1572872 | tf_op jit(solution)/shard_map/ppermute | solution.py:10
  84.1 9.4 %collective-permute-done.10 = f32[8,128,128]{2,0,1:T(8,128)} collective-permute-done((f32[8,128,128]{2,0,1:T(8,128)}, f32[8,128,128]{2,0,1:T(8,128)}, u32[]{:S(2)}, u32[]{:S(2)}) %collective-permute-start.10) | collective-permute-done | bytes 524320 | tf_op jit(solution)/shard_map/ppermute | solution.py:10
  93.4 1.4 fusion.65
  94.8 3.1 %collective-permute-done.11 = f32[8,128,128]{2,0,1:T(8,128)} collective-permute-done((f32[8,128,128]{2,0,1:T(8,128)}, f32[8,128,128]{2,0,1:T(8,128)}, u32[]{:S(2)}, u32[]{:S(2)}) %collective-permute-start.11) | collective-permute-done | bytes 524320 | tf_op jit(solution)/shard_map/ppermute | solution.py:10
  97.9 1.4 fusion.68
  99.4 1.4 convolution_add_fusion.1
  100.8 5.3 %collective-permute-done.9 = f32[8,128,128]{2,0,1:T(8,128)S(1)} collective-permute-done((f32[8,128,128]{2,0,1:T(8,128)S(1)}, f32[8,128,128]{2,0,1:T(8,128)S(1)}, u32[]{:S(2)}, u32[]{:S(2)}) %collective-permute-start.9) | collective-permute-done | bytes 524320 | tf_op jit(solution)/shard_map/ppermute | solution.py:10
  106.7 1.0 copy-done.2
  107.7 1.0 convolution_bitcast_fusion
  108.8 1.8 fusion.89
  110.6 52.1 %all-reduce.2.cloned.1.call-done = f32[512,128]{0,1:T(8,128)} async-done(((f32[512,128]{0,1:T(8,128)}), f32[512,128]{0,1:T(8,128)}) %all-reduce.2.cloned.1.call-update) | async-done | bytes 262160 | tf_op jit(solution)/shard_map/psum | solution.py:88
  162.7 1.8 copy.12
  164.5 43.6 %reduce-scatter.2.cloned.1.call-done = f32[1024,128]{1,0:T(8,128)} async-done(((f32[1024,512]{1,0:T(8,128)}), f32[1024,128]{1,0:T(8,128)}) %reduce-scatter.2.cloned.1.call-update) | async-done | bytes 524304 | tf_op jit(solution)/shard_map/reduce_scatter | solution.py:92
  208.1 1.8 convert_element_type.89
  (141 shorter events, 30.1 us)
Async XLA Ops:
  7.2 35.1 %copy-start = (bf16[512,128]{1,0:T(8,128)(2,1)S(1)}, bf16[512,128]{1,0:T(8,128)(2,1)}, u32[]{:S(2)}) copy-start(bf16[512,128]{1,0:T(8,128)(2,1)} %param.10) | copy-start | bytes 393220
  7.2 35.1 %all-gather.2.cloned.1.call-start = ((), (), s32[]{:S(2)}) async-start(), calls=%async_computation.1 | async-start | bytes 1310720 | tf_op jit(solution)/shard_map/all_gather | solution.py:28
  7.9 154.8 %all-reduce.2.cloned.1.call-start = ((), (), s32[]{:S(2)}) async-start(), calls=%async_computation.3 | async-start | bytes 524288 | tf_op jit(solution)/shard_map/psum | solution.py:88
  8.7 11.6 %collective-permute-start = (s32[8]{0:T(128)S(1)}, s32[8]{0:T(128)S(1)}, u32[]{:S(2)}, u32[]{:S(2)}) collective-permute-start(s32[8]{0:T(128)S(1)} %get-tuple-element.32), channel_id=1, source_target_pairs={{8,0},{12,4},{16,8},{20,12},{24,16},{28,20},{0,24},{4,28},{9,1},{1... | collective-permute-start | bytes 104 | tf_op jit(solution)/shard_map/ppermute | solution.py:10
  12.6 7.7 %collective-permute-start.2 = (s32[8]{0:T(128)S(1)}, s32[8]{0:T(128)S(1)}, u32[]{:S(2)}, u32[]{:S(2)}) collective-permute-start(s32[8]{0:T(128)S(1)} %get-tuple-element.31), channel_id=1, source_target_pairs={{4,0},{8,4},{12,8},{16,12},{20,16},{24,20},{28,24},{0,28},{5,1},{9... | collective-permute-start | bytes 104 | tf_op jit(solution)/shard_map/ppermute | solution.py:10
  12.6 7.7 %collective-permute-start.4 = (s32[8]{0:T(128)S(1)}, s32[8]{0:T(128)S(1)}, u32[]{:S(2)}, u32[]{:S(2)}) collective-permute-start(s32[8]{0:T(128)S(1)} %get-tuple-element.30), channel_id=1, source_target_pairs={{28,0},{0,4},{4,8},{8,12},{12,16},{16,20},{20,24},{24,28},{29,1},{... | collective-permute-start | bytes 104 | tf_op jit(solution)/shard_map/ppermute | solution.py:10
  13.1 7.8 %collective-permute-start.6 = (s32[8]{0:T(128)S(1)}, s32[8]{0:T(128)S(1)}, u32[]{:S(2)}, u32[]{:S(2)}) collective-permute-start(s32[8]{0:T(128)S(1)} %get-tuple-element.29), channel_id=1, source_target_pairs={{24,0},{28,4},{0,8},{4,12},{8,16},{12,20},{16,24},{20,28},{25,1},{... | collective-permute-start | bytes 104 | tf_op jit(solution)/shard_map/ppermute | solution.py:10
  20.2 25.7 %copy-start.19 = (s32[8]{0:T(128)}, s32[8]{0:T(128)S(1)}, u32[]{:S(2)}) copy-start(s32[8]{0:T(128)S(1)} %collective-permute-done) | copy-start | bytes 100
  20.3 25.7 %copy-start.27 = (s32[8]{0:T(128)}, s32[8]{0:T(128)S(1)}, u32[]{:S(2)}) copy-start(s32[8]{0:T(128)S(1)} %collective-permute-done.2) | copy-start | bytes 100
  20.3 25.7 %copy-start.23 = (s32[8]{0:T(128)}, s32[8]{0:T(128)S(1)}, u32[]{:S(2)}) copy-start(s32[8]{0:T(128)S(1)} %collective-permute-done.4) | copy-start | bytes 100
  20.9 25.0 %copy-start.21 = (s32[8]{0:T(128)}, s32[8]{0:T(128)S(1)}, u32[]{:S(2)}) copy-start(s32[8]{0:T(128)S(1)} %collective-permute-done.6) | copy-start | bytes 100
  22.6 23.4 %copy-start.1 = (bf16[1,5,8,128,128]{4,3,2,1,0:T(8,128)(2,1)S(1)}, bf16[1,5,8,128,128]{4,3,2,1,0:T(8,128)(2,1)}, u32[]{:S(2)}) copy-start(bf16[1,5,8,128,128]{4,3,2,1,0:T(8,128)(2,1)} %param.11) | copy-start | bytes 3932164
  44.6 10.8 %collective-permute-start.1 = (bf16[8,128,128]{2,1,0:T(8,128)(2,1)S(1)}, bf16[8,128,128]{2,1,0:T(8,128)(2,1)}, u32[]{:S(2)}, u32[]{:S(2)}) collective-permute-start(bf16[8,128,128]{2,1,0:T(8,128)(2,1)S(1)} %broadcast_select_fusion.3), channel_id=1, source_target_pairs={{24,0},{28,4},{0,8},{4,12},{8,16},{12,20},{16,24},{20,28},{25,1},{... | collective-permute-start | bytes 786440 | tf_op jit(solution)/shard_map/ppermute | solution.py:10
  46.7 6.2 %copy-start.25 = (pred[8]{0:T(512)(128)(4,1)S(1)}, pred[8]{0:T(512)(128)(4,1)}, u32[]{:S(2)}) copy-start(pred[8]{0:T(512)(128)(4,1)} %compare_and_fusion.5) | copy-start | bytes 28
  48.0 8.6 %collective-permute-start.3 = (bf16[8,128,128]{2,1,0:T(8,128)(2,1)S(1)}, bf16[8,128,128]{2,1,0:T(8,128)(2,1)}, u32[]{:S(2)}, u32[]{:S(2)}) collective-permute-start(bf16[8,128,128]{2,1,0:T(8,128)(2,1)S(1)} %broadcast_select_fusion.2), channel_id=1, source_target_pairs={{28,0},{0,4},{4,8},{8,12},{12,16},{16,20},{20,24},{24,28},{29,1},{... | collective-permute-start | bytes 786440 | tf_op jit(solution)/shard_map/ppermute | solution.py:10
  49.6 10.4 %collective-permute-start.5 = (bf16[8,128,128]{2,1,0:T(8,128)(2,1)}, bf16[8,128,128]{2,1,0:T(8,128)(2,1)}, u32[]{:S(2)}, u32[]{:S(2)}) collective-permute-start(bf16[8,128,128]{2,1,0:T(8,128)(2,1)} %broadcast_select_fusion.1), channel_id=1, source_target_pairs={{4,0},{8,4},{12,8},{16,12},{20,16},{24,20},{28,24},{0,28},{5,1},{9... | collective-permute-start | bytes 786440 | tf_op jit(solution)/shard_map/ppermute | solution.py:10
  53.7 10.4 %collective-permute-start.7 = (bf16[8,128,128]{2,1,0:T(8,128)(2,1)}, bf16[8,128,128]{2,1,0:T(8,128)(2,1)S(1)}, u32[]{:S(2)}, u32[]{:S(2)}) collective-permute-start(bf16[8,128,128]{2,1,0:T(8,128)(2,1)} %broadcast_select_fusion), channel_id=1, source_target_pairs={{8,0},{12,4},{16,8},{20,12},{24,16},{28,20},{0,24},{4,28},{9,1},{1... | collective-permute-start | bytes 786440 | tf_op jit(solution)/shard_map/ppermute | solution.py:10
  62.3 3.1 %copy-start.3 = (f32[8,128,128]{1,0,2:T(8,128)S(1)}, f32[8,128,128]{1,0,2:T(8,128)}, u32[]{:S(2)}) copy-start(f32[8,128,128]{1,0,2:T(8,128)} %copy.14) | copy-start | bytes 1572868
  70.9 3.7 %copy-start.16 = (pred[8]{0:T(512)(128)(4,1)S(1)}, pred[8]{0:T(512)(128)(4,1)}, u32[]{:S(2)}) copy-start(pred[8]{0:T(512)(128)(4,1)} %get-tuple-element.27) | copy-start | bytes 28
  71.9 27.5 %collective-permute-start.8 = (f32[8,128,128]{2,0,1:T(8,128)}, f32[8,128,128]{2,0,1:T(8,128)}, u32[]{:S(2)}, u32[]{:S(2)}) collective-permute-start(f32[8,128,128]{2,0,1:T(8,128)} %multiply_bitcast_fusion.3), channel_id=1, source_target_pairs={{8,0},{12,4},{16,8},{20,12},{24,16},{28,20},{0,24},{4,28},{9,1},{1... | collective-permute-start | bytes 1572872 | tf_op jit(solution)/shard_map/ppermute | solution.py:10
  76.2 17.2 %collective-permute-start.10 = (f32[8,128,128]{2,0,1:T(8,128)}, f32[8,128,128]{2,0,1:T(8,128)}, u32[]{:S(2)}, u32[]{:S(2)}) collective-permute-start(f32[8,128,128]{2,0,1:T(8,128)} %multiply_bitcast_fusion.1), channel_id=1, source_target_pairs={{28,0},{0,4},{4,8},{8,12},{12,16},{16,20},{20,24},{24,28},{29,1},{... | collective-permute-start | bytes 1572872 | tf_op jit(solution)/shard_map/ppermute | solution.py:10
  77.4 2.5 %copy-start.14 = (pred[8]{0:T(512)(128)(4,1)S(1)}, pred[8]{0:T(512)(128)(4,1)}, u32[]{:S(2)}) copy-start(pred[8]{0:T(512)(128)(4,1)} %get-tuple-element.23) | copy-start | bytes 28
  77.7 2.6 %copy-start.13 = (pred[8]{0:T(512)(128)(4,1)S(1)}, pred[8]{0:T(512)(128)(4,1)}, u32[]{:S(2)}) copy-start(pred[8]{0:T(512)(128)(4,1)} %get-tuple-element.7) | copy-start | bytes 28
  78.6 19.4 %collective-permute-start.11 = (f32[8,128,128]{2,0,1:T(8,128)}, f32[8,128,128]{2,0,1:T(8,128)}, u32[]{:S(2)}, u32[]{:S(2)}) collective-permute-start(f32[8,128,128]{2,0,1:T(8,128)} %multiply_bitcast_fusion), channel_id=1, source_target_pairs={{24,0},{28,4},{0,8},{4,12},{8,16},{12,20},{16,24},{20,28},{25,1},{... | collective-permute-start | bytes 1572872 | tf_op jit(solution)/shard_map/ppermute | solution.py:10
  80.8 2.8 %copy-start.8 = (pred[1,8]{1,0:T(4,128)(4,1)S(1)}, pred[1,8]{1,0:T(4,128)(4,1)}, u32[]{:S(2)}) copy-start(pred[1,8]{1,0:T(4,128)(4,1)} %get-tuple-element.34) | copy-start | bytes 28
  80.8 2.8 %copy-start.18 = (s32[1,8]{1,0:T(1,128)S(1)}, s32[1,8]{1,0:T(1,128)}, u32[]{:S(2)}) copy-start(s32[1,8]{1,0:T(1,128)} %slice.130) | copy-start | bytes 100
  81.0 12.4 %copy-start.24 = (s32[8]{0:T(128)S(1)}, s32[8]{0:T(128)}, u32[]{:S(2)}) copy-start(s32[8]{0:T(128)} %copy-done.23) | copy-start | bytes 100
  81.3 16.7 %copy-start.22 = (s32[8]{0:T(128)S(1)}, s32[8]{0:T(128)}, u32[]{:S(2)}) copy-start(s32[8]{0:T(128)} %copy-done.21) | copy-start | bytes 100
  81.3 24.8 %collective-permute-start.9 = (f32[8,128,128]{2,0,1:T(8,128)S(1)}, f32[8,128,128]{2,0,1:T(8,128)S(1)}, u32[]{:S(2)}, u32[]{:S(2)}) collective-permute-start(f32[8,128,128]{2,0,1:T(8,128)S(1)} %multiply_bitcast_fusion.2), channel_id=1, source_target_pairs={{4,0},{8,4},{12,8},{16,12},{20,16},{24,20},{28,24},{0,28},{5,1},{9... | collective-permute-start | bytes 1572872 | tf_op jit(solution)/shard_map/ppermute | solution.py:10
  84.1 15.3 %copy-start.20 = (s32[8]{0:T(128)S(1)}, s32[8]{0:T(128)}, u32[]{:S(2)}) copy-start(s32[8]{0:T(128)} %copy-done.19) | copy-start | bytes 100
  94.8 11.2 %copy-start.28 = (s32[8]{0:T(128)S(1)}, s32[8]{0:T(128)}, u32[]{:S(2)}) copy-start(s32[8]{0:T(128)} %copy-done.27) | copy-start | bytes 100
  108.8 99.3 %reduce-scatter.2.cloned.1.call-start = ((), (), s32[]{:S(2)}) async-start(), calls=%async_computation.2 | async-start | bytes 2621440 | tf_op jit(solution)/shard_map/reduce_scatter | solution.py:92
  (12 other events, 16.7 us)
Sparse Core Ops, SparseCore 0:
  9.5 32.6 all-gather.1
  108.9 53.7 all-reduce.1
  165.0 43.0 reduce-scatter.1
where the time goes:
time: 217 us; the launch traced here: 216 us
  waiting for transfers between devices  136 us (63%)
  local copies, waits for them, and re-layouts  19.5 us (9%)
  matrix products  17.6 us (8%)
  other arithmetic  14.8 us (7%)
  starting transfers between devices  14.4 us (7%)
  between operations  14.4 us (7%)
    psum x1, waiting for transfers between devices, on_device(): grad_w = lax.psum(weight_term, 'blk')  52.1 us
    reduce_scatter x1, waiting for transfers between devices, on_device(): lax.psum_scatter(partial_grad, 'feat', scatter_dimension=1, tiled=True)  43.6 us
    all_gather x1, waiting for transfers between devices, on_device(): full_feats = lax.all_gather(node_feats, 'feat', axis=1, tiled=True)  19.6 us
    ppermute x12, waiting for transfers between devices, shifted(): return lax.ppermute(block, axis, route)  19.6 us
    ppermute x12, starting transfers between devices, shifted(): return lax.ppermute(block, axis, route)  14.3 us
    unnamed x61, local copies, waits for them, and re-layouts  5.8 us
    dot_general x4, matrix products, on_device(): jnp.einsum('cs,sif->cif', target_onehot, received, precision=lax.Precisio...  4.6 us
  transfers between devices with their start and end apart: 15, of which 7 were waited for; matrix products, arithmetic and copies ran while one was open for 17% of the time, Pallas kernels for 0%

commit v1 on v0

--- a/solution.py
+++ b/solution.py
@@ -25,7 +25,10 @@
     col_onehot = (
         (tile_col[0][:, None, :] == block_ids[None, :, None]) & live_slots[:, None, :]
     ).astype(jnp.float32)
-    full_feats = lax.all_gather(node_feats, "feat", axis=1, tiled=True)
+    full_feats = jnp.concatenate(
+        lax.all_to_all(jnp.stack(lax.axis_size("feat") * [node_feats], axis=0), "feat", 0, 0),
+        axis=1,
+    )
     hidden = jnp.dot(full_feats, weight, preferred_element_type=jnp.float32).astype(jnp.bfloat16)
     panel_own = hidden.reshape(blocks, tile_side, feat_width)
     wanted_lists = {}

time: 217 us -> 182 us (0.84)
  waiting for transfers between devices: 136 us -> 74.6 us
  local copies, waits for them, and re-layouts: 19.5 us -> 26.6 us
  matrix products: 17.6 us -> 24.5 us
  starting transfers between devices: 14.4 us -> 19.9 us
  other arithmetic: 14.8 us -> 19.1 us
    reduce_scatter x1, waiting for transfers between devices: 43.6 us -> 0.01 us  [on_device(): lax.psum_scatter(partial_grad, 'feat', scatter_dimension=1, tiled=True)]
    all_gather x1 -> x0, waiting for transfers between devices: 19.6 us -> none  [on_device(): full_feats = lax.all_gather(node_feats, 'feat', axis=1, tiled=True)]
    all_to_all x0 -> x1, waiting for transfers between devices: none -> 16.3 us  [on_device(): lax.all_to_all(jnp.stack(lax.axis_size('feat') * [node_feats], axis=0), '...]
    ppermute x12, waiting for transfers between devices: 19.6 us -> 6.53 us  [shifted(): return lax.ppermute(block, axis, route)]
    all_to_all x0 -> x1, starting transfers between devices: none -> 6.48 us  [on_device(): lax.all_to_all(jnp.stack(lax.axis_size('feat') * [node_feats], axis=0), '...]
    dot_general x5, matrix products: 1.74 us -> 5.4 us  [slot_products(): jnp.einsum('sji,sjf->sif', tile_value[0, offset], picked, preferred_eleme...]
    dot_general x5, local copies, waits for them, and re-layouts: 1.16 us -> 4.51 us  [slot_products(): jnp.einsum('sji,sjf->sif', tile_value[0, offset], picked, preferred_eleme...]
    mul x4, other arithmetic: 2.8 us -> 5.93 us  [on_device(): slot_products(offset)]
  transfers between devices with their start and end apart: 15 -> 15, of which waited for: 7 -> 4; matrix products, arithmetic and copies ran while one was open for 17% -> 28% of each run, Pallas kernels for 0% -> 0%
where the time goes in v1:
time: 182 us; the launch traced here: 181 us
  waiting for transfers between devices  74.6 us (41%)
  local copies, waits for them, and re-layouts  26.6 us (15%)
  matrix products  24.5 us (13%)
  starting transfers between devices  19.9 us (11%)
  other arithmetic  19.1 us (10%)
  between operations  16 us (9%)
    psum x1, waiting for transfers between devices, on_device(): grad_w = lax.psum(weight_term, 'blk')  51.8 us
    all_to_all x1, waiting for transfers between devices, on_device(): lax.all_to_all(jnp.stack(lax.axis_size('feat') * [node_feats], axis=0), '...  16.3 us
    ppermute x12, starting transfers between devices, shifted(): return lax.ppermute(block, axis, route)  13.4 us
    ppermute x12, waiting for transfers between devices, shifted(): return lax.ppermute(block, axis, route)  6.53 us
    all_to_all x1, starting transfers between devices, on_device(): lax.all_to_all(jnp.stack(lax.axis_size('feat') * [node_feats], axis=0), '...  6.48 us
    dot_general x4, local copies, waits for them, and re-layouts, on_device(): jnp.einsum('sij,sjf->sif', tile_value[0, offset], arrived, preferred_elem...  6.13 us
    mul x4, other arithmetic, on_device(): slot_products(offset)  5.93 us
    gather x5, local copies, waits for them, and re-layouts, slot_products(): picked = jnp.take(grad_blocks, tile_row[0, offset], axis=0)  5.78 us
  transfers between devices with their start and end apart: 15, of which 4 were waited for; matrix products, arithmetic and copies ran while one was open for 28% of the time, Pallas kernels for 0%

profile of v1, /device:TPU:0, one launch (start us, length us, event | category | flops | bytes accessed | tf_op | source)
XLA Modules:
  0.0 180.8 jit_solution(8185122592657683556)
XLA Ops:
  10.3 6.5 %all-to-all-start = ((bf16[4,1024,128]{1,2,0:T(8,128)(2,1)}), bf16[4,1024,128]{1,2,0:T(8,128)(2,1)S(1)}, u32[]{:S(2)}, u32[]{:S(2)}) async-start(bf16[4,1024,128]{1,2,0:T(8,128)(2,1)} %stack.2), calls=%async_computation | async-start | bytes 2097152 | tf_op jit(solution)/shard_map/all_to_all | solution.py:29
  16.8 2.5 %collective-permute-start = (s32[8]{0:T(128)S(1)}, s32[8]{0:T(128)S(1)}, u32[]{:S(2)}, u32[]{:S(2)}) collective-permute-start(s32[8]{0:T(128)S(1)} %get-tuple-element.35), channel_id=1, source_target_pairs={{8,0},{12,4},{16,8},{20,12},{24,16},{28,20},{0,24},{4,28},{9,1},{1... | collective-permute-start | bytes 104 | tf_op jit(solution)/shard_map/ppermute | solution.py:10
  26.2 16.3 %all-to-all-done = bf16[4,1024,128]{1,2,0:T(8,128)(2,1)S(1)} async-done(((bf16[4,1024,128]{1,2,0:T(8,128)(2,1)}), bf16[4,1024,128]{1,2,0:T(8,128)(2,1)S(1)}, u32[]{:S(2)}, u32[]{:S(2)}) %all-to-all-start) | async-done | bytes 1048608 | tf_op jit(solution)/shard_map/all_to_all | solution.py:29
  44.4 1.5 collective-permute-start.1
  49.8 1.4 broadcast_select_fusion.2
  51.9 1.4 broadcast_select_fusion.1
  53.3 2.6 %collective-permute-start.5 = (bf16[8,128,128]{2,1,0:T(8,128)(2,1)}, bf16[8,128,128]{2,1,0:T(8,128)(2,1)}, u32[]{:S(2)}, u32[]{:S(2)}) collective-permute-start(bf16[8,128,128]{2,1,0:T(8,128)(2,1)} %broadcast_select_fusion.1), channel_id=1, source_target_pairs={{4,0},{8,4},{12,8},{16,12},{20,16},{24,20},{28,24},{0,28},{5,1},{9... | collective-permute-start | bytes 786440 | tf_op jit(solution)/shard_map/ppermute | solution.py:10
  56.6 1.4 broadcast_select_fusion
  61.0 2.1 %fusion.21 = f32[8,128,128]{2,1,0:T(8,128)} fusion(bf16[8,128,128]{2,1,0:T(8,128)(2,1)} %collective-permute-done.3, bf16[1,5,8,128,128]{4,3,2,1,0:T(8,128)(2,1)S(1)} %copy-done.1), kind=kOutput, calls=%fused_computation.48 | convolution fusion | flops 33554432 | bytes 1048576 | tf_op jit(solution)/shard_map/sij,sjf->sif/dot_general | solution.py:49
  64.1 2.1 %copy.19 = f32[8,128,128]{1,0,2:T(8,128)} copy(f32[8,128,128]{2,1,0:T(8,128)} %fusion.21) | data formatting | bytes 1048576 | tf_op jit(solution)/shard_map/sij,sjf->sif/dot_general | solution.py:49
  66.1 1.3 fusion.17
  69.5 2.0 %copy.21 = f32[8,128,128]{1,0,2:T(8,128)} copy(f32[8,128,128]{2,1,0:T(8,128)} %fusion.13) | data formatting | bytes 1048576 | tf_op jit(solution)/shard_map/sij,sjf->sif/dot_general | solution.py:49
  71.6 1.5 convolution_add_fusion.5
  78.3 1.9 %multiply_bitcast_fusion.3 = f32[8,128,128]{2,0,1:T(8,128)} fusion(f32[8,128,128]{1,0,2:T(8,128)} %copy.23, f32[8]{0:T(128)S(1)} %copy-done.13), kind=kLoop, calls=%fused_computation.34 | loop fusion | flops 131072 | bytes 1048608 | tf_op jit(solution)/shard_map/mul | solution.py:77
  80.2 2.5 %collective-permute-start.8 = (f32[8,128,128]{2,0,1:T(8,128)}, f32[8,128,128]{2,0,1:T(8,128)}, u32[]{:S(2)}, u32[]{:S(2)}) collective-permute-start(f32[8,128,128]{2,0,1:T(8,128)} %multiply_bitcast_fusion.3), channel_id=1, source_target_pairs={{8,0},{12,4},{16,8},{20,12},{24,16},{28,20},{0,24},{4,28},{9,1},{1... | collective-permute-start | bytes 1572872 | tf_op jit(solution)/shard_map/ppermute | solution.py:10
  83.3 1.4 gather_fusion.8
  84.7 1.3 fusion.15
  87.0 1.9 %multiply_bitcast_fusion.1 = f32[8,128,128]{2,0,1:T(8,128)} fusion(f32[8,128,128]{1,0,2:T(8,128)} %copy.25, f32[8]{0:T(128)S(1)} %copy-done.12), kind=kLoop, calls=%fused_computation.32 | loop fusion | flops 131072 | bytes 1048608 | tf_op jit(solution)/shard_map/mul | solution.py:77
  89.0 1.5 gather_fusion.9
  90.5 1.3 fusion.11
  92.8 1.9 %multiply_bitcast_fusion = f32[8,128,128]{2,0,1:T(8,128)} fusion(f32[8,128,128]{1,0,2:T(8,128)} %copy.26, f32[8]{0:T(128)S(1)} %copy-done.11), kind=kLoop, calls=%fused_computation.31 | loop fusion | flops 131072 | bytes 1048608 | tf_op jit(solution)/shard_map/mul | solution.py:77
  94.8 1.4 gather_fusion.7
  96.6 2.1 %fusion.19 = f32[8,128,128]{2,1,0:T(8,128)} fusion(bf16[8,128,128]{2,1,0:T(8,128)(2,1)} %gather_fusion.7, pred[8]{0:T(512)(128)(4,1)S(1)} %copy-done.14, bf16[1,5,8,128,128]{4,3,2,1,0:T(8,128)(2,1)S(1)} %copy-done.1), kind=kOutput, calls=%fused_computation.46 | convolution fusion | flops 33685504 | bytes 1049088 | tf_op jit(solution)/shard_map/sji,sjf->sif/dot_general | solution.py:64
  100.3 2.9 %collective-permute-start.9 = (f32[8,128,128]{2,0,1:T(8,128)S(1)}, f32[8,128,128]{2,0,1:T(8,128)S(1)}, u32[]{:S(2)}, u32[]{:S(2)}) collective-permute-start(f32[8,128,128]{2,0,1:T(8,128)S(1)} %multiply_bitcast_fusion.2), channel_id=1, source_target_pairs={{4,0},{8,4},{12,8},{16,12},{20,16},{24,20},{28,24},{0,28},{5,1},{9... | collective-permute-start | bytes 1572872 | tf_op jit(solution)/shard_map/ppermute | solution.py:10
  103.6 1.4 fusion.65
  105.0 5.8 %collective-permute-done.11 = f32[8,128,128]{2,0,1:T(8,128)} collective-permute-done((f32[8,128,128]{2,0,1:T(8,128)}, f32[8,128,128]{2,0,1:T(8,128)}, u32[]{:S(2)}, u32[]{:S(2)}) %collective-permute-start.11) | collective-permute-done | bytes 524320 | tf_op jit(solution)/shard_map/ppermute | solution.py:10
  110.8 1.4 fusion.68
  112.2 1.4 convolution_add_fusion.1
  116.2 1.8 fusion.89
  118.0 51.8 %all-reduce.2.cloned.1.call-done = f32[512,128]{0,1:T(8,128)} async-done(((f32[512,128]{0,1:T(8,128)}), f32[512,128]{0,1:T(8,128)}) %all-reduce.2.cloned.1.call-update) | async-done | bytes 262160 | tf_op jit(solution)/shard_map/psum | solution.py:91
  169.8 1.8 copy.16
  171.6 1.8 convert_element_type.89
  (142 shorter events, 35.0 us)
Async XLA Ops:
  8.0 34.5 %copy-start = (bf16[512,128]{1,0:T(8,128)(2,1)S(1)}, bf16[512,128]{1,0:T(8,128)(2,1)}, u32[]{:S(2)}) copy-start(bf16[512,128]{1,0:T(8,128)(2,1)} %param.10) | copy-start | bytes 393220
  10.3 6.5 %copy-start.8 = (s32[1,5,8]{2,0,1:T(1,128)S(1)}, s32[1,5,8]{2,0,1:T(1,128)}, u32[]{:S(2)}) copy-start(s32[1,5,8]{2,0,1:T(1,128)} %param.13) | copy-start | bytes 484
  10.3 9.9 %copy-start.7 = (s32[1,5,8]{2,0,1:T(1,128)S(1)}, s32[1,5,8]{2,0,1:T(1,128)}, u32[]{:S(2)}) copy-start(s32[1,5,8]{2,0,1:T(1,128)} %param.12) | copy-start | bytes 484
  10.3 10.5 %copy-start.28 = (s32[1,5]{1,0:T(1,128)S(1)}, s32[1,5]{1,0:T(1,128)}, u32[]{:S(2)}) copy-start(s32[1,5]{1,0:T(1,128)} %param.14) | copy-start | bytes 64
  10.3 32.2 %all-to-all-start = ((bf16[4,1024,128]{1,2,0:T(8,128)(2,1)}), bf16[4,1024,128]{1,2,0:T(8,128)(2,1)S(1)}, u32[]{:S(2)}, u32[]{:S(2)}) async-start(bf16[4,1024,128]{1,2,0:T(8,128)(2,1)} %stack.2), calls=%async_computation | async-start | bytes 2097152 | tf_op jit(solution)/shard_map/all_to_all | solution.py:29
  16.7 153.1 %all-reduce.2.cloned.1.call-start = ((), (), s32[]{:S(2)}) async-start(), calls=%async_computation.3 | async-start | bytes 524288 | tf_op jit(solution)/shard_map/psum | solution.py:91
  16.8 6.6 %collective-permute-start = (s32[8]{0:T(128)S(1)}, s32[8]{0:T(128)S(1)}, u32[]{:S(2)}, u32[]{:S(2)}) collective-permute-start(s32[8]{0:T(128)S(1)} %get-tuple-element.35), channel_id=1, source_target_pairs={{8,0},{12,4},{16,8},{20,12},{24,16},{28,20},{0,24},{4,28},{9,1},{1... | collective-permute-start | bytes 104 | tf_op jit(solution)/shard_map/ppermute | solution.py:10
  19.3 4.1 %collective-permute-start.2 = (s32[8]{0:T(128)S(1)}, s32[8]{0:T(128)S(1)}, u32[]{:S(2)}, u32[]{:S(2)}) collective-permute-start(s32[8]{0:T(128)S(1)} %get-tuple-element.34), channel_id=1, source_target_pairs={{4,0},{8,4},{12,8},{16,12},{20,16},{24,20},{28,24},{0,28},{5,1},{9... | collective-permute-start | bytes 104 | tf_op jit(solution)/shard_map/ppermute | solution.py:10
  19.3 4.7 %collective-permute-start.4 = (s32[8]{0:T(128)S(1)}, s32[8]{0:T(128)S(1)}, u32[]{:S(2)}, u32[]{:S(2)}) collective-permute-start(s32[8]{0:T(128)S(1)} %get-tuple-element.33), channel_id=1, source_target_pairs={{28,0},{0,4},{4,8},{8,12},{12,16},{16,20},{20,24},{24,28},{29,1},{... | collective-permute-start | bytes 104 | tf_op jit(solution)/shard_map/ppermute | solution.py:10
  19.8 4.8 %collective-permute-start.6 = (s32[8]{0:T(128)S(1)}, s32[8]{0:T(128)S(1)}, u32[]{:S(2)}, u32[]{:S(2)}) collective-permute-start(s32[8]{0:T(128)S(1)} %get-tuple-element.32), channel_id=1, source_target_pairs={{24,0},{28,4},{0,8},{4,12},{8,16},{12,20},{16,24},{20,28},{25,1},{... | collective-permute-start | bytes 104 | tf_op jit(solution)/shard_map/ppermute | solution.py:10
  23.3 23.2 %copy-start.20 = (s32[8]{0:T(128)}, s32[8]{0:T(128)S(1)}, u32[]{:S(2)}) copy-start(s32[8]{0:T(128)S(1)} %collective-permute-done) | copy-start | bytes 100
  23.3 23.1 %copy-start.26 = (s32[8]{0:T(128)}, s32[8]{0:T(128)S(1)}, u32[]{:S(2)}) copy-start(s32[8]{0:T(128)S(1)} %collective-permute-done.2) | copy-start | bytes 100
  24.0 22.5 %copy-start.24 = (s32[8]{0:T(128)}, s32[8]{0:T(128)S(1)}, u32[]{:S(2)}) copy-start(s32[8]{0:T(128)S(1)} %collective-permute-done.4) | copy-start | bytes 100
  24.6 21.9 %copy-start.22 = (s32[8]{0:T(128)}, s32[8]{0:T(128)S(1)}, u32[]{:S(2)}) copy-start(s32[8]{0:T(128)S(1)} %collective-permute-done.6) | copy-start | bytes 100
  42.5 4.0 %copy-start.1 = (bf16[1,5,8,128,128]{4,3,2,1,0:T(8,128)(2,1)S(1)}, bf16[1,5,8,128,128]{4,3,2,1,0:T(8,128)(2,1)}, u32[]{:S(2)}) copy-start(bf16[1,5,8,128,128]{4,3,2,1,0:T(8,128)(2,1)} %param.11) | copy-start | bytes 3932164
  44.4 15.3 %collective-permute-start.1 = (bf16[8,128,128]{2,1,0:T(8,128)(2,1)}, bf16[8,128,128]{2,1,0:T(8,128)(2,1)}, u32[]{:S(2)}, u32[]{:S(2)}) collective-permute-start(bf16[8,128,128]{2,1,0:T(8,128)(2,1)} %broadcast_select_fusion.3), channel_id=1, source_target_pairs={{24,0},{28,4},{0,8},{4,12},{8,16},{12,20},{16,24},{20,28},{25,1},{... | collective-permute-start | bytes 786440 | tf_op jit(solution)/shard_map/ppermute | solution.py:10
  51.2 9.8 %collective-permute-start.3 = (bf16[8,128,128]{2,1,0:T(8,128)(2,1)}, bf16[8,128,128]{2,1,0:T(8,128)(2,1)}, u32[]{:S(2)}, u32[]{:S(2)}) collective-permute-start(bf16[8,128,128]{2,1,0:T(8,128)(2,1)} %broadcast_select_fusion.2), channel_id=1, source_target_pairs={{28,0},{0,4},{4,8},{8,12},{12,16},{16,20},{20,24},{24,28},{29,1},{... | collective-permute-start | bytes 786440 | tf_op jit(solution)/shard_map/ppermute | solution.py:10
  53.3 12.8 %collective-permute-start.5 = (bf16[8,128,128]{2,1,0:T(8,128)(2,1)}, bf16[8,128,128]{2,1,0:T(8,128)(2,1)}, u32[]{:S(2)}, u32[]{:S(2)}) collective-permute-start(bf16[8,128,128]{2,1,0:T(8,128)(2,1)} %broadcast_select_fusion.1), channel_id=1, source_target_pairs={{4,0},{8,4},{12,8},{16,12},{20,16},{24,20},{28,24},{0,28},{5,1},{9... | collective-permute-start | bytes 786440 | tf_op jit(solution)/shard_map/ppermute | solution.py:10
  58.0 10.4 %collective-permute-start.7 = (bf16[8,128,128]{2,1,0:T(8,128)(2,1)}, bf16[8,128,128]{2,1,0:T(8,128)(2,1)S(1)}, u32[]{:S(2)}, u32[]{:S(2)}) collective-permute-start(bf16[8,128,128]{2,1,0:T(8,128)(2,1)} %broadcast_select_fusion), channel_id=1, source_target_pairs={{8,0},{12,4},{16,8},{20,12},{24,16},{28,20},{0,24},{4,28},{9,1},{1... | collective-permute-start | bytes 786440 | tf_op jit(solution)/shard_map/ppermute | solution.py:10
  78.3 6.4 %copy-start.17 = (pred[8]{0:T(512)(128)(4,1)S(1)}, pred[8]{0:T(512)(128)(4,1)}, u32[]{:S(2)}) copy-start(pred[8]{0:T(512)(128)(4,1)} %get-tuple-element.30) | copy-start | bytes 28
  80.2 32.0 %collective-permute-start.8 = (f32[8,128,128]{2,0,1:T(8,128)}, f32[8,128,128]{2,0,1:T(8,128)}, u32[]{:S(2)}, u32[]{:S(2)}) collective-permute-start(f32[8,128,128]{2,0,1:T(8,128)} %multiply_bitcast_fusion.3), channel_id=1, source_target_pairs={{8,0},{12,4},{16,8},{20,12},{24,16},{28,20},{0,24},{4,28},{9,1},{1... | collective-permute-start | bytes 1572872 | tf_op jit(solution)/shard_map/ppermute | solution.py:10
  83.3 3.7 %copy-start.12 = (f32[8]{0:T(128)S(1)}, f32[8]{0:T(128)}, u32[]{:S(2)}) copy-start(f32[8]{0:T(128)} %get-tuple-element.39) | copy-start | bytes 100
  86.0 4.5 %copy-start.16 = (pred[8]{0:T(512)(128)(4,1)S(1)}, pred[8]{0:T(512)(128)(4,1)}, u32[]{:S(2)}) copy-start(pred[8]{0:T(512)(128)(4,1)} %get-tuple-element.28) | copy-start | bytes 28
  89.0 14.6 %collective-permute-start.10 = (f32[8,128,128]{2,0,1:T(8,128)}, f32[8,128,128]{2,0,1:T(8,128)}, u32[]{:S(2)}, u32[]{:S(2)}) collective-permute-start(f32[8,128,128]{2,0,1:T(8,128)} %multiply_bitcast_fusion.1), channel_id=1, source_target_pairs={{28,0},{0,4},{4,8},{8,12},{12,16},{16,20},{20,24},{24,28},{29,1},{... | collective-permute-start | bytes 1572872 | tf_op jit(solution)/shard_map/ppermute | solution.py:10
  89.0 3.9 %copy-start.11 = (f32[8]{0:T(128)S(1)}, f32[8]{0:T(128)}, u32[]{:S(2)}) copy-start(f32[8]{0:T(128)} %get-tuple-element.38) | copy-start | bytes 100
  91.8 4.4 %copy-start.15 = (pred[8]{0:T(512)(128)(4,1)S(1)}, pred[8]{0:T(512)(128)(4,1)}, u32[]{:S(2)}) copy-start(pred[8]{0:T(512)(128)(4,1)} %get-tuple-element.26) | copy-start | bytes 28
  94.8 16.0 %collective-permute-start.11 = (f32[8,128,128]{2,0,1:T(8,128)}, f32[8,128,128]{2,0,1:T(8,128)}, u32[]{:S(2)}, u32[]{:S(2)}) collective-permute-start(f32[8,128,128]{2,0,1:T(8,128)} %multiply_bitcast_fusion), channel_id=1, source_target_pairs={{24,0},{28,4},{0,8},{4,12},{8,16},{12,20},{16,24},{20,28},{25,1},{... | collective-permute-start | bytes 1572872 | tf_op jit(solution)/shard_map/ppermute | solution.py:10
  100.3 10.5 %copy-start.23 = (s32[8]{0:T(128)S(1)}, s32[8]{0:T(128)}, u32[]{:S(2)}) copy-start(s32[8]{0:T(128)} %copy-done.22) | copy-start | bytes 100
  100.3 14.0 %collective-permute-start.9 = (f32[8,128,128]{2,0,1:T(8,128)S(1)}, f32[8,128,128]{2,0,1:T(8,128)S(1)}, u32[]{:S(2)}, u32[]{:S(2)}) collective-permute-start(f32[8,128,128]{2,0,1:T(8,128)S(1)} %multiply_bitcast_fusion.2), channel_id=1, source_target_pairs={{4,0},{8,4},{12,8},{16,12},{20,16},{24,20},{28,24},{0,28},{5,1},{9... | collective-permute-start | bytes 1572872 | tf_op jit(solution)/shard_map/ppermute | solution.py:10
  103.6 8.6 %copy-start.21 = (s32[8]{0:T(128)S(1)}, s32[8]{0:T(128)}, u32[]{:S(2)}) copy-start(s32[8]{0:T(128)} %copy-done.20) | copy-start | bytes 100
  105.0 9.4 %copy-start.27 = (s32[8]{0:T(128)S(1)}, s32[8]{0:T(128)}, u32[]{:S(2)}) copy-start(s32[8]{0:T(128)} %copy-done.26) | copy-start | bytes 100
  116.2 55.4 %reduce-scatter.2.cloned.1.call-start = ((), (), s32[]{:S(2)}) async-start(), calls=%async_computation.2 | async-start | bytes 2621440 | tf_op jit(solution)/shard_map/reduce_scatter | solution.py:95
  (12 other events, 29.8 us)
Sparse Core Ops, SparseCore 0:
  116.3 53.4 all-reduce.1
Sparse Core Ops, SparseCore 1:
  119.0 43.1 reduce-scatter.1
